TPU v7x, 32 devices: a whole 2x2x4 slice. The times are simulated.
32 devices in a mesh: section: 2 (over core), ep: 4 (over z), tp: 4 (over y, x).
Axes of the slice: x: 2, y: 2, z: 4, core: 2. Of those that a mesh axis runs over, the one named last changes fastest.
Arguments:
- hidden: bfloat16 [512, 6144], P('ep', ('section', 'tp')), may hold values from -6 to 6
- expert_ids: int32 [512, 2], P('ep'), may hold values from 0 to 7, all different within a row; in each aligned block of 128 rows (0 to 127, 128 to 255, ...) at most 40 rows name the same one
- gate_weights: float32 [512, 2], P('ep'), may hold values from 0 to 1, as said below
- gate_proj: bfloat16 [4, 6144, 16384], P('ep', None, ('section', 'tp')), may hold values from -0.078125 to 0.078125
- up_proj: bfloat16 [4, 6144, 16384], P('ep', None, ('section', 'tp')), may hold values from -0.078125 to 0.078125
- down_proj: bfloat16 [4, 6144, 16384], P('ep', ('section', 'tp')), may hold values from -0.0625 to 0.0625
Outputs:
- moe_out: bfloat16 [512, 6144], P('ep', ('section', 'tp'))
Inputs may be any that keep to these rules, and one draw needn't show every extreme that they name: `expert_ids`: the two entries of a row differ. Within the 128 rows of one device no expert is named by more than 40 rows, and in some device's rows one expert is named by exactly 40. Every expert is named somewhere. `gate_weights`: the two weights of a token are positive, sum to one, and the first is at least the second.
All inputs are finite; a program needn't handle non-finite values.
Results may differ from a plain program's by a relative error of at most 0.0059.
Values may be sent and summed in bfloat16 or wider, within the bound.
A program may use at most 192 MiB of HBM per device.

v0:
```python
import jax
import jax.numpy as jnp
from jax import lax
from jax.sharding import PartitionSpec as P

E = 8
F = 8192
CAP = 40


def slot_tables(expert_ids, capacity, experts):
    token_count = expert_ids.shape[0]
    flat_ids = expert_ids.reshape(-1)
    onehot = (flat_ids[:, None] == jnp.arange(experts, dtype=jnp.int32)[None, :]).astype(jnp.int32)
    before = jnp.cumsum(onehot, axis=0) - onehot
    position = jnp.sum(before * onehot, axis=1)
    slot_of = (flat_ids * capacity + position).reshape(token_count, -1)
    slot_range = jnp.arange(experts * capacity, dtype=jnp.int32)
    matches_st = slot_of[None, :, :] == slot_range[:, None, None]
    dispatch = jnp.any(matches_st, axis=2).astype(jnp.bfloat16)
    return (dispatch, slot_of)


def on_device(hidden, expert_ids, gate_weights, gate_proj, up_proj, down_proj):
    ep_count = lax.axis_size("ep")
    share_count = lax.axis_size("section") * lax.axis_size("tp")
    owners_each = max(1, ep_count // E)
    experts_each = max(1, E // ep_count)
    local_cols = gate_proj.shape[2]
    group_cols = local_cols * share_count
    owner_index = lax.axis_index("ep")
    share_index = lax.axis_index("section") * lax.axis_size("tp") + lax.axis_index("tp")
    own_expert = (owner_index * group_cols + share_index * local_cols) // F
    slot_expert = owner_index // owners_each * experts_each + jnp.arange(
        experts_each, dtype=jnp.int32
    )
    keep_mask = (slot_expert == own_expert).reshape(1, experts_each, 1, 1)
    gate_local = gate_proj[0]
    up_local = up_proj[0]
    down_local = down_proj[0]
    dispatch, slot_of = slot_tables(expert_ids, CAP, E)
    packed = jnp.dot(
        dispatch,
        lax.all_gather(hidden, ("section", "tp"), axis=1, tiled=True),
        preferred_element_type=jnp.float32,
    ).astype(jnp.bfloat16)
    grouped = packed.reshape(E // experts_each, experts_each, CAP, packed.shape[1])
    received = lax.all_to_all(
        jnp.repeat(grouped, owners_each, axis=0), "ep", split_axis=0, concat_axis=0, tiled=True
    )
    flat_rows = received.reshape(-1, received.shape[3])
    gate_out = jnp.dot(flat_rows, gate_local, preferred_element_type=jnp.float32)
    up_out = jnp.dot(flat_rows, up_local, preferred_element_type=jnp.float32)
    lead_shape = received.shape[:3]
    activated = (jax.nn.silu(gate_out) * up_out).reshape(lead_shape + (local_cols,))
    activated = jnp.where(keep_mask, activated, 0.0).astype(jnp.bfloat16)
    flat_act = activated.reshape(-1, local_cols)
    outputs = lax.dot_general(
        lax.all_gather(flat_act, ("section", "tp"), axis=1, tiled=True),
        down_local,
        (((1,), (1,)), ((), ())),
        preferred_element_type=jnp.float32,
    )
    outputs = outputs.reshape(lead_shape + (down_local.shape[0],)).astype(jnp.bfloat16)
    returned = lax.all_to_all(outputs, "ep", split_axis=0, concat_axis=0, tiled=True)
    grouped = returned.astype(jnp.float32).reshape(
        E // experts_each, owners_each, experts_each, CAP, returned.shape[3]
    )
    summed = jnp.sum(grouped, axis=1).reshape(E * CAP, returned.shape[3])
    first_rows = summed[slot_of[:, 0]]
    second_rows = summed[slot_of[:, 1]]
    combined_out = gate_weights[:, 0:1] * first_rows + gate_weights[:, 1:2] * second_rows
    return combined_out.astype(jnp.bfloat16)


def on_device_paired(hidden, expert_ids, gate_weights, gate_proj, up_proj, down_proj):
    ep_count = lax.axis_size("ep")
    pair = lax.axis_size("section")
    width = hidden.shape[1]
    local_cols = gate_proj.shape[2]
    dispatch, slot_of = slot_tables(expert_ids, CAP, E)
    packed = jnp.dot(dispatch, hidden, preferred_element_type=jnp.float32).astype(jnp.bfloat16)
    sent = packed.reshape(ep_count, pair, CAP, width)
    received = lax.all_to_all(sent, "ep", split_axis=0, concat_axis=0, tiled=True)
    swapped = lax.all_to_all(received, "section", split_axis=1, concat_axis=1, tiled=True)
    halves = lax.all_gather(swapped, "tp", axis=0)
    rows = jnp.transpose(halves, (1, 3, 2, 0, 4)).reshape(ep_count * CAP, -1)
    gate_out = jnp.dot(rows, gate_proj[0], preferred_element_type=jnp.float32)
    up_out = jnp.dot(rows, up_proj[0], preferred_element_type=jnp.float32)
    activated = (jax.nn.silu(gate_out) * up_out).astype(jnp.bfloat16)
    gathered = lax.all_gather(activated, "tp", axis=1, tiled=True)
    both = lax.all_gather(gathered, "section", axis=0)
    outputs = jnp.stack(
        [
            lax.dot_general(
                both[i],
                down_proj[0][:, i * F : (i + 1) * F],
                (((1,), (1,)), ((), ())),
                preferred_element_type=jnp.float32,
            )
            .astype(jnp.bfloat16)
            .reshape(ep_count, CAP, width)
            for i in range(pair)
        ],
        axis=1,
    )
    returned = lax.all_to_all(outputs, "ep", split_axis=0, concat_axis=0, tiled=True)
    flat = returned.reshape(E * CAP, width)
    slot_range = jnp.arange(E * CAP, dtype=jnp.int32)[None, :]
    picks = [(slot_of[:, k : k + 1] == slot_range).astype(jnp.bfloat16) for k in range(2)]
    first_rows, second_rows = [jnp.dot(p, flat, preferred_element_type=jnp.float32) for p in picks]
    combined = gate_weights[:, 0:1] * first_rows + gate_weights[:, 1:2] * second_rows
    return combined.astype(jnp.bfloat16)


def solution(mesh):

    def body(*args):
        paired = (
            E // mesh.shape["ep"] == mesh.shape["section"]
            and args[3].shape[2] * mesh.shape["tp"] == F
        )
        return (on_device_paired if paired else on_device)(*args)

    return jax.shard_map(
        body,
        mesh=mesh,
        in_specs=(
            P("ep", ("section", "tp")),
            P("ep", None),
            P("ep", None),
            P("ep", None, ("section", "tp")),
            P("ep", None, ("section", "tp")),
            P("ep", ("section", "tp"), None),
        ),
        out_specs=P("ep", ("section", "tp")),
        check_vma=False,
    )
```

profile of v0, /device:TPU:0, one launch (start us, length us, event | category | flops | bytes accessed | tf_op | source)
XLA Modules:
  0.0 201.5 jit_solution(15060545460979945678)
XLA Ops:
  6.5 0.8 copy.49
  7.4 0.1 eq.72
  7.5 0.1 eq.68
  7.7 0.6 reduce-window.6
  8.2 0.2 slice_reduce_fusion
  8.5 0.1 fusion.32
  8.6 0.1 reduce_sum.12
  8.7 0.1 copy.51
  8.8 0.7 multiply_add_fusion
  9.6 0.3 convolution_convert_fusion
  9.8 19.9 %all_to_all.15 = bf16[4,2,40,768]{3,2,1,0:T(8,128)(2,1)S(1)} all-to-all(bf16[4,2,40,768]{3,2,1,0:T(8,128)(2,1)S(1)} %bitcast.47), channel_id=1, replica_groups=mesh['section'=2,'ep'=4,'tp'=4] {'ep'}, dimensions={0} | all-to-all | bytes 983040 | tf_op jit(solution)/shard_map/all_to_all | solution.py:84
  29.8 4.1 %all_to_all.16 = bf16[4,2,40,768]{3,2,0,1:T(8,128)(2,1)S(1)} all-to-all(bf16[4,2,40,768]{3,2,0,1:T(8,128)(2,1)S(1)} %copy.52), channel_id=1, replica_groups=mesh['section'=2,'ep'=4,'tp'=4] {'section'}, dimensions={1} | all-to-all | bytes 983040 | tf_op jit(solution)/shard_map/all_to_all | solution.py:85
  33.9 0.8 copy.53
  34.7 0.0 all-gather.8.cloned.1.call-update
  34.7 0.0 all-gather.6.cloned.1.call-start
  34.8 33.4 %all-gather.8.cloned.1.call-done = bf16[16,2,40,768]{3,2,1,0:T(8,128)(2,1)} async-done(((bf16[4,2,40,768]{3,2,1,0:T(8,128)(2,1)}), bf16[16,2,40,768]{3,2,1,0:T(8,128)(2,1)}) %all-gather.8.cloned.1.call-update) | async-done | bytes 1966096 | tf_op jit(solution)/shard_map/all_gather | solution.py:86
  68.2 3.1 %copy.54 = bf16[4,40,2,4,768]{4,3,2,1,0:T(4,128)(2,1)S(1)} copy(bf16[4,40,2,4,768]{4,1,2,0,3:T(8,128)(2,1)} %bitcast.46) | data formatting | bytes 3932160 | tf_op jit(solution)/shard_map/transpose | solution.py:87
  71.3 2.4 %reshape.37 = bf16[160,6144]{1,0:T(8,128)(2,1)} reshape(bf16[4,40,2,4,768]{4,3,2,1,0:T(4,128)(2,1)S(1)} %copy.54) | data formatting | bytes 3932160 | tf_op jit(solution)/shard_map/reshape | solution.py:87
  73.8 12.9 %fusion.2 = f32[160,2048]{1,0:T(8,128)S(1)} fusion(bf16[160,6144]{1,0:T(8,128)(2,1)} %reshape.37, bf16[1,6144,2048]{2,1,0:T(8,128)(2,1)} %param.9), kind=kOutput, calls=%fused_computation.2 | convolution fusion | flops 4026531840 | bytes 28442624 | tf_op jit(solution)/shard_map/dot_general | solution.py:88
  86.7 11.6 %fusion.13 = bf16[160,2048]{1,0:T(8,128)(2,1)} fusion(bf16[160,6144]{1,0:T(8,128)(2,1)S(1)} %copy-done.2, bf16[1,6144,2048]{2,1,0:T(8,128)(2,1)} %param.10, f32[160,2048]{1,0:T(8,128)S(1)} %fusion.2), kind=kOutput, calls=%fused_computation.11 | convolution fusion | flops 4028497920 | bytes 29097984 | tf_op jit(solution)/shard_map/dot_general | solution.py:89
  98.3 0.0 all-gather.6.cloned.1.call-update
  98.3 0.2 all-gather.10.cloned.1.call-start
  98.5 39.6 %all-gather.6.cloned.1.call-done = bf16[160,8192]{1,0:T(8,128)(2,1)} async-done(((bf16[160,2048]{1,0:T(8,128)(2,1)}), bf16[160,8192]{1,0:T(8,128)(2,1)}) %all-gather.6.cloned.1.call-update) | async-done | bytes 2621456 | tf_op jit(solution)/shard_map/all_gather | solution.py:91
  138.1 0.0 all-gather.10.cloned.1.call-update
  138.1 16.8 %all-gather.10.cloned.1.call-done = bf16[320,8192]{1,0:T(8,128)(2,1)} async-done(((bf16[160,8192]{1,0:T(8,128)(2,1)}), bf16[320,8192]{1,0:T(8,128)(2,1)}) %all-gather.10.cloned.1.call-update) | async-done | bytes 5242896 | tf_op jit(solution)/shard_map/all_gather | solution.py:92
  154.9 9.8 %fusion.17 = bf16[160,768]{1,0:T(8,128)(2,1)S(1)} fusion(bf16[768,16384]{1,0:T(8,128)(2,1)} %bitcast.50, bf16[320,8192]{1,0:T(8,128)(2,1)} %all-gather.10.cloned.1.call-done), kind=kOutput, calls=%fused_computation.16 | convolution fusion | flops 2013388800 | bytes 15450112 | tf_op jit(solution)/shard_map/dot_general | solution.py:95
  164.7 8.9 %fusion.22 = bf16[160,768]{1,0:T(8,128)(2,1)S(1)} fusion(bf16[768,16384]{1,0:T(8,128)(2,1)} %bitcast.51, bf16[320,8192]{1,0:T(8,128)(2,1)S(1)} %copy-done.4), kind=kOutput, calls=%fused_computation.17 | convolution fusion | flops 2013388800 | bytes 15450112 | tf_op jit(solution)/shard_map/dot_general | solution.py:95
  173.7 0.8 pad_maximum_fusion
  174.5 4.9 %all-to-all-start.2 = ((bf16[4,2,40,768]{3,2,1,0:T(8,128)(2,1)}), bf16[4,2,40,768]{3,2,1,0:T(8,128)(2,1)S(1)}, u32[]{:S(2)}, u32[]{:S(2)}) async-start(bf16[4,2,40,768]{3,2,1,0:T(8,128)(2,1)} %pad_maximum_fusion), calls=%async_computation.2 | async-start | bytes 983040 | tf_op jit(solution)/shard_map/all_to_all | solution.py:107
  179.4 14.2 %all-to-all-done.2 = bf16[4,2,40,768]{3,2,1,0:T(8,128)(2,1)S(1)} async-done(((bf16[4,2,40,768]{3,2,1,0:T(8,128)(2,1)}), bf16[4,2,40,768]{3,2,1,0:T(8,128)(2,1)S(1)}, u32[]{:S(2)}, u32[]{:S(2)}) %all-to-all-start.2) | async-done | bytes 491552 | tf_op jit(solution)/shard_map/all_to_all | solution.py:107
  193.6 0.3 convolution_multiply_fusion
  193.9 1.0 fusion.27
  (18 shorter events, 0.2 us)
Async XLA Ops:
  6.5 3.0 %copy-start = (bf16[128,768]{1,0:T(8,128)(2,1)S(1)}, bf16[128,768]{1,0:T(8,128)(2,1)}, u32[]{:S(2)}) copy-start(bf16[128,768]{1,0:T(8,128)(2,1)} %param.6) | copy-start | bytes 589828
  6.5 61.7 %all-gather.8.cloned.1.call-start = ((), (), s32[]{:S(2)}) async-start(), calls=%async_computation.4 | async-start | bytes 2457600 | tf_op jit(solution)/shard_map/all_gather | solution.py:86
  34.7 103.4 %all-gather.6.cloned.1.call-start = ((), (), s32[]{:S(2)}) async-start(), calls=%async_computation.3 | async-start | bytes 3276800 | tf_op jit(solution)/shard_map/all_gather | solution.py:91
  73.8 12.9 %copy-start.2 = (bf16[160,6144]{1,0:T(8,128)(2,1)S(1)}, bf16[160,6144]{1,0:T(8,128)(2,1)}, u32[]{:S(2)}) copy-start(bf16[160,6144]{1,0:T(8,128)(2,1)} %reshape.37) | copy-start | bytes 5898244
  98.3 56.6 %all-gather.10.cloned.1.call-start = ((), (), s32[]{:S(2)}) async-start(), calls=%async_computation.5 | async-start | bytes 7864320 | tf_op jit(solution)/shard_map/all_gather | solution.py:92
  154.9 9.8 %copy-start.4 = (bf16[320,8192]{1,0:T(8,128)(2,1)S(1)}, bf16[320,8192]{1,0:T(8,128)(2,1)}, u32[]{:S(2)}) copy-start(bf16[320,8192]{1,0:T(8,128)(2,1)} %all-gather.10.cloned.1.call-done) | copy-start | bytes 15728644
  164.7 14.7 %copy-start.3 = (f32[128,2]{0,1:T(2,128)S(1)}, f32[128,2]{0,1:T(2,128)}, u32[]{:S(2)}) copy-start(f32[128,2]{0,1:T(2,128)} %param.8) | copy-start | bytes 3076
  164.7 30.2 %copy-start.1 = (bf16[128,768]{1,0:T(8,128)(2,1)S(1)}, bf16[128,768]{1,0:T(8,128)(2,1)}, u32[]{:S(2)}) copy-start(bf16[128,768]{1,0:T(8,128)(2,1)} %param.6) | copy-start | bytes 589828
  174.5 19.1 %all-to-all-start.2 = ((bf16[4,2,40,768]{3,2,1,0:T(8,128)(2,1)}), bf16[4,2,40,768]{3,2,1,0:T(8,128)(2,1)S(1)}, u32[]{:S(2)}, u32[]{:S(2)}) async-start(bf16[4,2,40,768]{3,2,1,0:T(8,128)(2,1)} %pad_maximum_fusion), calls=%async_computation.2 | async-start | bytes 983040 | tf_op jit(solution)/shard_map/all_to_all | solution.py:107
Sparse Core Ops, SparseCore 0:
  34.9 33.3 all-gather.7
  98.4 39.6 all-gather.5
  139.7 15.2 all-gather.9
where the time goes:
time: 202 us; the launch traced here: 201 us
  waiting for transfers between devices  104 us (51%)
  matrix products  44.8 us (22%)
  blocking collectives  24 us (12%)
  between operations  13.2 us (7%)
  local copies, waits for them, and re-layouts  7.91 us (4%)
  starting transfers between devices  5.12 us (3%)
  other arithmetic  2.28 us (1%)
    all_gather x1, waiting for transfers between devices, on_device_paired(): gathered = lax.all_gather(activated, 'tp', axis=1, tiled=True)  39.6 us
    all_gather x1, waiting for transfers between devices, on_device_paired(): halves = lax.all_gather(swapped, 'tp', axis=0)  33.4 us
    all_to_all x1, blocking collectives, on_device_paired(): lax.all_to_all(sent, 'ep', split_axis=0, concat_axis=0, tiled=True)  19.9 us
    dot_general x2, matrix products, on_device_paired(): lax.dot_general(both[i], down_proj[0][:, i * F:(i + 1) * F], (((1,), (1,)...  18.7 us
    all_gather x1, waiting for transfers between devices, on_device_paired(): both = lax.all_gather(gathered, 'section', axis=0)  16.8 us
    all_to_all x1, waiting for transfers between devices, on_device_paired(): lax.all_to_all(outputs, 'ep', split_axis=0, concat_axis=0, tiled=True)  14.2 us
    dot_general x1, matrix products, on_device_paired(): gate_out = jnp.dot(rows, gate_proj[0], preferred_element_type=jnp.float32)  12.9 us
    dot_general x1, matrix products, on_device_paired(): up_out = jnp.dot(rows, up_proj[0], preferred_element_type=jnp.float32)  11.6 us
  transfers between devices with their start and end apart: 4, of which 4 were waited for; matrix products, arithmetic and copies ran while one was open for 0% of the time, Pallas kernels for 0%

commit v1 on v0

--- a/solution.py
+++ b/solution.py
@@ -6,6 +6,12 @@
 E = 8
 F = 8192
 CAP = 40
+
+
+def laid_out(blocks, dim):
+    shape = list(blocks.shape[1:])
+    shape[dim] *= blocks.shape[0]
+    return jnp.moveaxis(blocks, 0, dim).reshape(shape)
 
 
 def slot_tables(expert_ids, capacity, experts):
@@ -88,7 +94,19 @@
     gate_out = jnp.dot(rows, gate_proj[0], preferred_element_type=jnp.float32)
     up_out = jnp.dot(rows, up_proj[0], preferred_element_type=jnp.float32)
     activated = (jax.nn.silu(gate_out) * up_out).astype(jnp.bfloat16)
-    gathered = lax.all_gather(activated, "tp", axis=1, tiled=True)
+    size = lax.axis_size("tp")
+    pairs = [(i_2, (i_2 + 1) % size) for i_2 in range(size)]
+    back = [(b, a) for a, b in pairs]
+    lower, upper = ([], [])
+    for turn in range(size - 1):
+        if turn % 2 == 0:
+            lower.append(lax.ppermute(lower[-1] if lower else activated, "tp", pairs))
+        else:
+            upper.append(lax.ppermute(upper[-1] if upper else activated, "tp", back))
+    parts = jnp.stack([*lower[::-1], activated, *upper])
+    shift = lax.axis_index("tp") - len(lower)
+    parts = parts[(jnp.arange(size) - shift) % size]
+    gathered = laid_out(parts, 1)
     both = lax.all_gather(gathered, "section", axis=0)
     outputs = jnp.stack(
         [

time: 202 us -> 218 us (1.079)
  local copies, waits for them, and re-layouts: 7.91 us -> 18.4 us
  starting transfers between devices: 5.12 us -> 8.44 us
    ppermute x0 -> x3, waiting for transfers between devices: none -> 41.9 us  [the longest x2 28.5 us: on_device_paired(): lower.append(lax.ppermute(lower[-1] if lower else activated, 'tp', pairs))]
    all_gather x1 -> x0, waiting for transfers between devices: 39.6 us -> none  [on_device_paired(): gathered = lax.all_gather(activated, 'tp', axis=1, tiled=True)]
    transpose x0 -> x1, local copies, waits for them, and re-layouts: none -> 3.76 us  [laid_out(): return jnp.moveaxis(blocks, 0, dim).reshape(shape)]
    another operation x1 -> x2, local copies, waits for them, and re-layouts: 0.01 us -> 3.59 us  [the longest x1 3.59 us: on_device_paired(): both = lax.all_gather(gathered, 'section', axis=0)]
    ppermute x0 -> x3, starting transfers between devices: none -> 3.54 us  [the longest x2 2.08 us: on_device_paired(): lower.append(lax.ppermute(lower[-1] if lower else activated, 'tp', pairs))]
    gather x0 -> x1, local copies, waits for them, and re-layouts: none -> 2.24 us  [on_device_paired(): parts = parts[(jnp.arange(size) - shift) % size]]
  transfers between devices with their start and end apart: 4 -> 6, of which waited for: 4 -> 6; matrix products, arithmetic and copies ran while one was open for 0% -> 0% of each run, Pallas kernels for 0% -> 0%
where the time goes in v1:
time: 218 us; the launch traced here: 217 us
  waiting for transfers between devices  105 us (48%)
  matrix products  44 us (20%)
  blocking collectives  24 us (11%)
  local copies, waits for them, and re-layouts  18.4 us (8%)
  between operations  13.5 us (6%)
  starting transfers between devices  8.44 us (4%)
  other arithmetic  4.12 us (2%)
    all_gather x1, waiting for transfers between devices, on_device_paired(): halves = lax.all_gather(swapped, 'tp', axis=0)  33.4 us
    ppermute x2, waiting for transfers between devices, on_device_paired(): lower.append(lax.ppermute(lower[-1] if lower else activated, 'tp', pairs))  28.5 us
    all_to_all x1, blocking collectives, on_device_paired(): lax.all_to_all(sent, 'ep', split_axis=0, concat_axis=0, tiled=True)  19.9 us
    dot_general x2, matrix products, on_device_paired(): lax.dot_general(both[i], down_proj[0][:, i * F:(i + 1) * F], (((1,), (1,)...  18.7 us
    all_gather x1, waiting for transfers between devices, on_device_paired(): both = lax.all_gather(gathered, 'section', axis=0)  15.4 us
    all_to_all x1, waiting for transfers between devices, on_device_paired(): lax.all_to_all(outputs, 'ep', split_axis=0, concat_axis=0, tiled=True)  14.2 us
    ppermute x1, waiting for transfers between devices, on_device_paired(): upper.append(lax.ppermute(upper[-1] if upper else activated, 'tp', back))  13.5 us
    dot_general x1, matrix products, on_device_paired(): gate_out = jnp.dot(rows, gate_proj[0], preferred_element_type=jnp.float32)  12.9 us
  transfers between devices with their start and end apart: 6, of which 6 were waited for; matrix products, arithmetic and copies ran while one was open for 0% of the time, Pallas kernels for 0%

profile of v1, /device:TPU:0, one launch (start us, length us, event | category | flops | bytes accessed | tf_op | source)
XLA Modules:
  0.0 217.5 jit_solution(8398614679854551324)
XLA Ops:
  6.5 0.8 copy.54
  7.7 0.6 reduce-window.6
  8.2 0.2 slice_reduce_fusion
  8.8 0.7 multiply_add_fusion
  9.6 0.3 convolution_convert_fusion
  9.8 19.9 %all_to_all.15 = bf16[4,2,40,768]{3,2,1,0:T(8,128)(2,1)S(1)} all-to-all(bf16[4,2,40,768]{3,2,1,0:T(8,128)(2,1)S(1)} %bitcast.65), channel_id=1, replica_groups=mesh['section'=2,'ep'=4,'tp'=4] {'ep'}, dimensions={0} | all-to-all | bytes 983040 | tf_op jit(solution)/shard_map/all_to_all | solution.py:90
  29.8 4.1 %all_to_all.16 = bf16[4,2,40,768]{3,2,0,1:T(8,128)(2,1)S(1)} all-to-all(bf16[4,2,40,768]{3,2,0,1:T(8,128)(2,1)S(1)} %copy.57), channel_id=1, replica_groups=mesh['section'=2,'ep'=4,'tp'=4] {'section'}, dimensions={1} | all-to-all | bytes 983040 | tf_op jit(solution)/shard_map/all_to_all | solution.py:91
  33.9 0.8 copy.58
  34.8 33.4 %all-gather.6.cloned.1.call-done = bf16[16,2,40,768]{3,2,1,0:T(8,128)(2,1)} async-done(((bf16[4,2,40,768]{3,2,1,0:T(8,128)(2,1)}), bf16[16,2,40,768]{3,2,1,0:T(8,128)(2,1)}) %all-gather.6.cloned.1.call-update) | async-done | bytes 1966096 | tf_op jit(solution)/shard_map/all_gather | solution.py:92
  68.2 3.1 %copy.59 = bf16[4,40,2,4,768]{4,3,2,1,0:T(4,128)(2,1)S(1)} copy(bf16[4,40,2,4,768]{4,1,2,0,3:T(8,128)(2,1)} %bitcast.64) | data formatting | bytes 3932160 | tf_op jit(solution)/shard_map/transpose | solution.py:93
  71.3 2.5 %reshape.86 = bf16[160,6144]{1,0:T(8,128)(2,1)} reshape(bf16[4,40,2,4,768]{4,3,2,1,0:T(4,128)(2,1)S(1)} %copy.59) | data formatting | bytes 3932160 | tf_op jit(solution)/shard_map/reshape | solution.py:93
  73.8 12.9 %fusion.2 = f32[160,2048]{1,0:T(8,128)S(1)} fusion(bf16[160,6144]{1,0:T(8,128)(2,1)} %reshape.86, bf16[1,6144,2048]{2,1,0:T(8,128)(2,1)} %param.9), kind=kOutput, calls=%fused_computation.3 | convolution fusion | flops 4026531840 | bytes 28442624 | tf_op jit(solution)/shard_map/dot_general | solution.py:94
  86.7 10.8 %fusion.11 = bf16[160,2048]{1,0:T(8,128)(2,1)S(1)} fusion(bf16[160,6144]{1,0:T(8,128)(2,1)S(1)} %copy-done.2, bf16[1,6144,2048]{2,1,0:T(8,128)(2,1)} %param.10, f32[160,2048]{1,0:T(8,128)S(1)} %fusion.2), kind=kOutput, calls=%fused_computation.13 | convolution fusion | flops 4028497920 | bytes 29097984 | tf_op jit(solution)/shard_map/dot_general | solution.py:95
  97.5 1.5 collective-permute-start
  99.0 1.5 collective-permute-start.2
  100.4 15.6 %collective-permute-done = bf16[160,2048]{1,0:T(8,128)(2,1)S(1)} collective-permute-done((bf16[160,2048]{1,0:T(8,128)(2,1)S(1)}, bf16[160,2048]{1,0:T(8,128)(2,1)S(1)}, u32[]{:S(2)}, u32[]{:S(2)}) %collective-permute-start) | collective-permute-done | bytes 655392 | tf_op jit(solution)/shard_map/ppermute | solution.py:103
  116.0 0.6 collective-permute-start.1
  116.6 13.5 %collective-permute-done.2 = bf16[160,2048]{1,0:T(8,128)(2,1)S(1)} collective-permute-done((bf16[160,2048]{1,0:T(8,128)(2,1)S(1)}, bf16[160,2048]{1,0:T(8,128)(2,1)S(1)}, u32[]{:S(2)}, u32[]{:S(2)}) %collective-permute-start.2) | collective-permute-done | bytes 655392 | tf_op jit(solution)/shard_map/ppermute | solution.py:105
  130.1 12.9 %collective-permute-done.1 = bf16[160,2048]{1,0:T(8,128)(2,1)S(1)} collective-permute-done((bf16[160,2048]{1,0:T(8,128)(2,1)S(1)}, bf16[160,2048]{1,0:T(8,128)(2,1)S(1)}, u32[]{:S(2)}, u32[]{:S(2)}) %collective-permute-start.1) | collective-permute-done | bytes 655392 | tf_op jit(solution)/shard_map/ppermute | solution.py:103
  143.0 0.9 copy-done.5
  143.9 1.8 pad_maximum_fusion
  145.7 2.2 %gather_fusion = bf16[4,160,2048]{2,1,0:T(8,128)(2,1)} fusion(bf16[4,160,2048]{2,1,0:T(8,128)(2,1)S(1)} %pad_maximum_fusion, s32[1024]{0:T(1024)S(1)} %pad_clamp_fusion), kind=kCustom, calls=%fused_computation | custom fusion | bytes 5242896 | tf_op jit(solution)/shard_map/gather | solution.py:108
  147.9 3.8 %copy.60 = bf16[160,4,2048]{2,1,0:T(4,128)(2,1)S(1)} copy(bf16[160,4,2048]{2,0,1:T(8,128)(2,1)} %bitcast.61) | data formatting | bytes 5242880 | tf_op jit(solution)/shard_map/transpose | solution.py:14
  151.7 3.6 %all_gather_reshape.3 = bf16[1,160,8192]{2,1,0:T(8,128)(2,1)} reshape(bf16[160,4,2048]{2,1,0:T(4,128)(2,1)S(1)} %copy.60) | data formatting | bytes 5242880 | tf_op jit(solution)/shard_map/all_gather;reshape | solution.py:110
  155.3 15.4 %all-gather.4.cloned.1.call-done = bf16[2,160,8192]{2,1,0:T(8,128)(2,1)} async-done(((bf16[1,160,8192]{2,1,0:T(8,128)(2,1)}), bf16[2,160,8192]{2,1,0:T(8,128)(2,1)}) %all-gather.4.cloned.1.call-update) | async-done | bytes 5242896 | tf_op jit(solution)/shard_map/all_gather | solution.py:110
  170.7 9.8 %fusion.15 = bf16[160,768]{1,0:T(8,128)(2,1)S(1)} fusion(bf16[768,16384]{1,0:T(8,128)(2,1)} %bitcast.72, bf16[2,160,8192]{2,1,0:T(8,128)(2,1)} %all-gather.4.cloned.1.call-done), kind=kOutput, calls=%fused_computation.18 | convolution fusion | flops 2013388800 | bytes 15450112 | tf_op jit(solution)/shard_map/dot_general | solution.py:113
  180.5 8.9 %fusion.18 = bf16[160,768]{1,0:T(8,128)(2,1)S(1)} fusion(bf16[768,16384]{1,0:T(8,128)(2,1)} %bitcast.73, bf16[2,160,8192]{2,1,0:T(8,128)(2,1)S(1)} %copy-done.7), kind=kOutput, calls=%fused_computation.19 | convolution fusion | flops 2013388800 | bytes 15450112 | tf_op jit(solution)/shard_map/dot_general | solution.py:113
  189.4 0.8 pad_maximum_fusion.1
  190.2 4.9 %all-to-all-start.2 = ((bf16[4,2,40,768]{3,2,1,0:T(8,128)(2,1)}), bf16[4,2,40,768]{3,2,1,0:T(8,128)(2,1)S(1)}, u32[]{:S(2)}, u32[]{:S(2)}) async-start(bf16[4,2,40,768]{3,2,1,0:T(8,128)(2,1)} %pad_maximum_fusion.1), calls=%async_computation.2 | async-start | bytes 983040 | tf_op jit(solution)/shard_map/all_to_all | solution.py:125
  195.1 14.2 %all-to-all-done.2 = bf16[4,2,40,768]{3,2,1,0:T(8,128)(2,1)S(1)} async-done(((bf16[4,2,40,768]{3,2,1,0:T(8,128)(2,1)}), bf16[4,2,40,768]{3,2,1,0:T(8,128)(2,1)S(1)}, u32[]{:S(2)}, u32[]{:S(2)}) %all-to-all-start.2) | async-done | bytes 491552 | tf_op jit(solution)/shard_map/all_to_all | solution.py:125
  209.3 0.3 convolution_multiply_fusion
  209.7 1.0 fusion.21
  (33 shorter events, 0.8 us)
Async XLA Ops:
  6.5 3.0 %copy-start = (bf16[128,768]{1,0:T(8,128)(2,1)S(1)}, bf16[128,768]{1,0:T(8,128)(2,1)}, u32[]{:S(2)}) copy-start(bf16[128,768]{1,0:T(8,128)(2,1)} %param.6) | copy-start | bytes 589828
  6.5 61.7 %all-gather.6.cloned.1.call-start = ((), (), s32[]{:S(2)}) async-start(), calls=%async_computation.4 | async-start | bytes 2457600 | tf_op jit(solution)/shard_map/all_gather | solution.py:92
  34.7 135.9 %all-gather.4.cloned.1.call-start = ((), (), s32[]{:S(2)}) async-start(), calls=%async_computation.3 | async-start | bytes 7864320 | tf_op jit(solution)/shard_map/all_gather | solution.py:110
  73.8 12.9 %copy-start.2 = (bf16[160,6144]{1,0:T(8,128)(2,1)S(1)}, bf16[160,6144]{1,0:T(8,128)(2,1)}, u32[]{:S(2)}) copy-start(bf16[160,6144]{1,0:T(8,128)(2,1)} %reshape.86) | copy-start | bytes 5898244
  97.5 18.6 %collective-permute-start = (bf16[160,2048]{1,0:T(8,128)(2,1)S(1)}, bf16[160,2048]{1,0:T(8,128)(2,1)S(1)}, u32[]{:S(2)}, u32[]{:S(2)}) collective-permute-start(bf16[160,2048]{1,0:T(8,128)(2,1)S(1)} %fusion.11), channel_id=1, source_target_pairs={{0,1},{1,2},{2,3},{3,0},{4,5},{5,6},{6,7},{7,4},{8,9},{9,10},{10,1... | collective-permute-start | bytes 1966088 | tf_op jit(solution)/shard_map/ppermute | solution.py:103
  99.0 31.1 %collective-permute-start.2 = (bf16[160,2048]{1,0:T(8,128)(2,1)S(1)}, bf16[160,2048]{1,0:T(8,128)(2,1)S(1)}, u32[]{:S(2)}, u32[]{:S(2)}) collective-permute-start(bf16[160,2048]{1,0:T(8,128)(2,1)S(1)} %fusion.11), channel_id=1, source_target_pairs={{1,0},{2,1},{3,2},{0,3},{5,4},{6,5},{7,6},{4,7},{9,8},{10,9},{11,1... | collective-permute-start | bytes 1966088 | tf_op jit(solution)/shard_map/ppermute | solution.py:105
  116.0 26.9 %copy-start.3 = (bf16[160,2048]{1,0:T(8,128)(2,1)}, bf16[160,2048]{1,0:T(8,128)(2,1)S(1)}, u32[]{:S(2)}) copy-start(bf16[160,2048]{1,0:T(8,128)(2,1)S(1)} %collective-permute-done) | copy-start | bytes 1966084
  116.0 26.9 %collective-permute-start.1 = (bf16[160,2048]{1,0:T(8,128)(2,1)S(1)}, bf16[160,2048]{1,0:T(8,128)(2,1)S(1)}, u32[]{:S(2)}, u32[]{:S(2)}) collective-permute-start(bf16[160,2048]{1,0:T(8,128)(2,1)S(1)} %collective-permute-done), channel_id=1, source_target_pairs={{0,1},{1,2},{2,3},{3,0},{4,5},{5,6},{6,7},{7,4},{8,9},{9,10},{10,1... | collective-permute-start | bytes 1966088 | tf_op jit(solution)/shard_map/ppermute | solution.py:103
  130.1 12.9 %copy-start.4 = (bf16[160,2048]{1,0:T(8,128)(2,1)}, bf16[160,2048]{1,0:T(8,128)(2,1)S(1)}, u32[]{:S(2)}) copy-start(bf16[160,2048]{1,0:T(8,128)(2,1)S(1)} %collective-permute-done.2) | copy-start | bytes 1966084
  143.0 0.9 copy-start.5
  170.7 9.8 %copy-start.7 = (bf16[2,160,8192]{2,1,0:T(8,128)(2,1)S(1)}, bf16[2,160,8192]{2,1,0:T(8,128)(2,1)}, u32[]{:S(2)}) copy-start(bf16[2,160,8192]{2,1,0:T(8,128)(2,1)} %all-gather.4.cloned.1.call-done) | copy-start | bytes 15728644
  180.5 14.6 %copy-start.6 = (f32[128,2]{0,1:T(2,128)S(1)}, f32[128,2]{0,1:T(2,128)}, u32[]{:S(2)}) copy-start(f32[128,2]{0,1:T(2,128)} %param.8) | copy-start | bytes 3076
  180.5 30.2 %copy-start.1 = (bf16[128,768]{1,0:T(8,128)(2,1)S(1)}, bf16[128,768]{1,0:T(8,128)(2,1)}, u32[]{:S(2)}) copy-start(bf16[128,768]{1,0:T(8,128)(2,1)} %param.6) | copy-start | bytes 589828
  190.2 19.1 %all-to-all-start.2 = ((bf16[4,2,40,768]{3,2,1,0:T(8,128)(2,1)}), bf16[4,2,40,768]{3,2,1,0:T(8,128)(2,1)S(1)}, u32[]{:S(2)}, u32[]{:S(2)}) async-start(bf16[4,2,40,768]{3,2,1,0:T(8,128)(2,1)} %pad_maximum_fusion.1), calls=%async_computation.2 | async-start | bytes 983040 | tf_op jit(solution)/shard_map/all_to_all | solution.py:125
Sparse Core Ops, SparseCore 0:
  34.9 33.3 all-gather.5
  155.4 15.1 all-gather.3
